TPU v7x, 32 devices: a whole 2x2x4 slice. The times are simulated.
32 devices in a mesh: req: 8 (over z, y), tp: 4 (over x, core).
Axes of the slice: x: 2, y: 2, z: 4, core: 2. Of those that a mesh axis runs over, the one named last changes fastest.
Arguments:
- tokens: bfloat16 [4096, 2048], P('req')
- token_request_number: int32 [8, 512], P('req'), may hold values from 0 to 7, never falling along the last dimension, each value on 1 to 256 neighbouring positions
- request_adapter_position: int32 [8, 8], P('req'), may hold values from 0 to 15
- adapters_in_use: int32 [16], replicated, may hold values from 0 to 15, as said below
- adapter_storage_slot: int32 [16], replicated, may hold values from 0 to 15, each once
- input_norm_gain: bfloat16 [2048], replicated, may hold values from 0.5 to 1.5
- query_weight: bfloat16 [2048, 2048], P('req', 'tp')
- key_weight: bfloat16 [2048, 2048], P('req', 'tp')
- value_weight: bfloat16 [2048, 2048], P('req', 'tp'), may hold values from -0.125 to 0.125
- output_weight: bfloat16 [2048, 2048], P('tp', 'req'), may hold values from -0.125 to 0.125
- adapter_down_weight: bfloat16 [16, 2, 16, 2048], P('req'), may hold values from -0.125 to 0.125
- adapter_up_weight: bfloat16 [16, 2, 16, 2048], P('req', None, None, 'tp'), may hold values from -0.75 to 0.75
Outputs:
- layer_out: bfloat16 [4096, 2048], P('req', 'tp')
Inputs may be any that keep to these rules, and one draw needn't show every extreme that they name: `adapters_in_use`: 16 different adapter numbers; 0 and 15 are always among them. `token_request_number`: the 512 tokens of each index of req form exactly 8 requests in order, each of 1 to 256 tokens, and one of exactly 256.
All inputs are finite; a program needn't handle non-finite values.
Results may differ from a plain program's by a relative error of at most 0.01.
Values may be sent and summed in bfloat16 or wider, within the bound.
A program may use at most 64 MiB of HBM per device.

v0:
```python
import jax
import jax.numpy as jnp
from jax import lax
from jax.sharding import PartitionSpec as P

HEAD_WIDTH = 64
norm_eps = 1e-05
rope_base = 130000.0
adapter_scale = 2.0


def fetch_adapters(down_part, up_part, active_slots, request_adapters, req_total):
    slot_total = down_part.shape[0]
    stored = jnp.concatenate([down_part, up_part], axis=1)
    split = down_part.shape[1]
    if slot_total * req_total <= 2 * active_slots.shape[0]:
        fetched = lax.all_gather(stored, "req", axis=0, tiled=True)
        places = active_slots[request_adapters]
    else:
        own = active_slots // slot_total == lax.axis_index("req")
        rows = jnp.where(
            own[:, None],
            jnp.take(stored, active_slots % slot_total, axis=0),
            jnp.zeros((), stored.dtype),
        )
        fetched = lax.psum(rows, "req")
        places = request_adapters
    return (fetched[:, :split], fetched[:, split:], places)


def positions_of(segment):
    ordinal = jnp.arange(segment.shape[0], dtype=jnp.int32)
    starts = jnp.concatenate([jnp.ones((1,), jnp.bool_), segment[1:] != segment[:-1]])
    segment_start = lax.cummax(jnp.where(starts, ordinal, jnp.zeros_like(ordinal)), axis=0)
    return ordinal - segment_start


def apply_rotation(values, token_positions):
    half_dim = HEAD_WIDTH // 2
    frequency = rope_base ** (-(jnp.arange(half_dim, dtype=jnp.float32) * 2.0 / HEAD_WIDTH))
    angles = token_positions.astype(jnp.float32)[:, None] * frequency[None, :]
    cosine = jnp.cos(angles)[:, None, :]
    sine_part = jnp.sin(angles)[:, None, :]
    first_half = values[..., :half_dim]
    second_half = values[..., half_dim:]
    return jnp.concatenate(
        [
            first_half * cosine - second_half * sine_part,
            second_half * cosine + first_half * sine_part,
        ],
        axis=-1,
    )


def attend(query_per_head, key_heads, value_per_head, segment):
    scores = (
        jnp.einsum("qhd,khd->hqk", query_per_head, key_heads, preferred_element_type=jnp.float32)
        * 0.125
    )
    ordinal = jnp.arange(segment.shape[0], dtype=jnp.int32)
    allowed = (segment[:, None] == segment[None, :]) & (ordinal[None, :] <= ordinal[:, None])
    scores = jnp.where(allowed[None], scores, jnp.float32(-1e30))
    row_peak = jnp.max(scores, axis=-1, keepdims=True)
    exponent = jnp.where(allowed[None], jnp.exp(scores - row_peak), jnp.float32(0.0))
    weights = (exponent / jnp.sum(exponent, axis=-1, keepdims=True)).astype(jnp.bfloat16)
    return jnp.einsum(
        "hqk,khd->qhd", weights, value_per_head, preferred_element_type=jnp.float32
    ).astype(jnp.bfloat16)


def local(
    tokens,
    token_request_number,
    request_adapter_position,
    adapters_in_use,
    adapter_storage_slot,
    input_norm_gain,
    query_weight,
    key_weight,
    value_weight,
    output_weight,
    adapter_down_weight,
    adapter_up_weight,
):
    row_total, model_width = tokens.shape
    local_width = query_weight.shape[1]
    reduced_rows = adapter_down_weight.shape[2]
    active_count = adapters_in_use.shape[0]
    slot_total = adapter_down_weight.shape[0]
    segment = token_request_number[0]
    request_adapters = request_adapter_position[0]
    tp_total = lax.axis_size("tp")
    req_total = lax.axis_size("req")
    part_rows = reduced_rows // tp_total
    down_part = lax.dynamic_slice_in_dim(
        adapter_down_weight, lax.axis_index("tp") * part_rows, part_rows, 2
    ).reshape(slot_total, 2 * part_rows * model_width)
    up_part = adapter_up_weight.reshape(slot_total, 2 * reduced_rows * local_width)
    down_all, up_all, request_places = fetch_adapters(
        down_part,
        up_part,
        jnp.take(adapter_storage_slot, adapters_in_use, axis=0),
        request_adapters,
        req_total,
    )
    place_total = down_all.shape[0]
    floats = tokens.astype(jnp.float32)
    normed = (
        floats
        * lax.rsqrt(jnp.mean(floats * floats, axis=-1, keepdims=True) + norm_eps)
        * input_norm_gain.astype(jnp.float32)
    ).astype(jnp.bfloat16)
    query_plain = jnp.dot(
        normed,
        lax.all_gather(query_weight, "req", axis=0, tiled=True),
        preferred_element_type=jnp.float32,
    )
    key_base = jnp.dot(
        normed,
        lax.all_gather(key_weight, "req", axis=0, tiled=True),
        preferred_element_type=jnp.float32,
    )
    value_plain = jnp.dot(
        normed,
        lax.all_gather(value_weight, "req", axis=0, tiled=True),
        preferred_element_type=jnp.float32,
    )
    request_total = request_adapters.shape[0]
    member = segment[:, None] == jnp.arange(request_total, dtype=jnp.int32)[None, :]
    token_place = jnp.sum(
        jnp.where(member, request_places[None, :], jnp.zeros_like(request_places)[None, :]), axis=1
    )
    share = 2 * part_rows
    shrunk_all = lax.dot_general(
        normed,
        down_all.reshape(place_total * share, model_width),
        (((1,), (1,)), ((), ())),
        preferred_element_type=jnp.float32,
    ).astype(jnp.bfloat16)
    column = jnp.arange(place_total * share, dtype=jnp.int32)
    kept = jnp.where(
        token_place[:, None] == (column // share)[None, :], shrunk_all, jnp.zeros((), jnp.bfloat16)
    )
    fold = (column % share)[:, None] == jnp.arange(share, dtype=jnp.int32)[None, :]
    shrunk_part = jnp.dot(
        kept, fold.astype(jnp.bfloat16), preferred_element_type=jnp.float32
    ).astype(jnp.bfloat16)
    shrunk = lax.all_gather(shrunk_part, "tp", axis=1, tiled=True)
    source = jnp.arange(tp_total * share, dtype=jnp.int32)
    source_kind = source % share // part_rows
    source_rank = source // share * part_rows + source % part_rows
    target = jnp.arange(place_total * reduced_rows, dtype=jnp.int32)
    mine = token_place[:, None] == (target // reduced_rows)[None, :]
    up_all = up_all.reshape(place_total, 2, reduced_rows, local_width)

    def change_of(kind):
        spread_map = (source_kind == kind)[:, None] & (
            source_rank[:, None] == (target % reduced_rows)[None, :]
        )
        spread = jnp.dot(
            shrunk, spread_map.astype(jnp.bfloat16), preferred_element_type=jnp.float32
        ).astype(jnp.bfloat16)
        spread = jnp.where(mine, spread, jnp.zeros((), jnp.bfloat16))
        return jnp.dot(
            spread,
            up_all[:, kind].reshape(place_total * reduced_rows, local_width),
            preferred_element_type=jnp.float32,
        )

    query_change = change_of(0)
    value_change = change_of(1)
    head_total = local_width // HEAD_WIDTH
    token_positions = positions_of(segment)
    query_per_head = apply_rotation(
        (query_plain + adapter_scale * query_change).reshape(row_total, head_total, HEAD_WIDTH),
        token_positions,
    ).astype(jnp.bfloat16)
    key_heads = apply_rotation(
        key_base.reshape(row_total, head_total, HEAD_WIDTH), token_positions
    ).astype(jnp.bfloat16)
    value_per_head = (
        (value_plain + adapter_scale * value_change)
        .astype(jnp.bfloat16)
        .reshape(row_total, head_total, HEAD_WIDTH)
    )
    attended = attend(query_per_head, key_heads, value_per_head, segment).reshape(
        row_total, local_width
    )
    partial_out = jnp.dot(
        attended,
        lax.all_gather(output_weight, "req", axis=1, tiled=True),
        preferred_element_type=jnp.float32,
    )
    summed = lax.psum_scatter(
        partial_out.astype(jnp.bfloat16), "tp", scatter_dimension=1, tiled=True
    ).astype(jnp.float32)
    share_width = summed.shape[1]
    residual_part = lax.dynamic_slice_in_dim(
        tokens, lax.axis_index("tp") * share_width, share_width, 1
    )
    return (summed + residual_part.astype(jnp.float32)).astype(jnp.bfloat16)


def solution(mesh):
    in_specs = (
        P("req", None),
        P("req", None),
        P("req", None),
        P(),
        P(),
        P(),
        P("req", "tp"),
        P("req", "tp"),
        P("req", "tp"),
        P("tp", "req"),
        P("req", None, None, None),
        P("req", None, None, "tp"),
    )
    out_specs = P("req", "tp")
    return jax.shard_map(local, mesh=mesh, in_specs=in_specs, out_specs=out_specs, check_vma=False)
```

profile of v0, /device:TPU:0, one launch (start us, length us, event | category | flops | bytes accessed | tf_op | source)
XLA Modules:
  0.0 296.7 jit_solution(14154784594400048160)
XLA Ops:
  6.6 1.0 copy.18
  12.0 2.1 fusion.2
  15.6 0.9 fusion.18
  17.9 0.9 multiply_cosine_fusion
  18.9 33.5 %all-gather.15.cloned.1.call-done = bf16[8,2,32768]{2,1,0:T(2,128)(2,1)} async-done(((bf16[1,2,32768]{2,1,0:T(2,128)(2,1)}), bf16[8,2,32768]{2,1,0:T(2,128)(2,1)}) %all-gather.15.cloned.1.call-update) | async-done | bytes 1048592 | tf_op jit(solution)/shard_map/all_gather | solution.py:17
  52.4 1.5 reshape.319
  55.8 1.3 reshape.294
  57.0 0.9 fusion.17
  58.0 5.4 %all_gather.20 = bf16[512,32]{0,1:T(8,128)(2,1)S(1)} all-gather(bf16[512,8]{0,1:T(8,128)(2,1)S(1)} %fusion.17), channel_id=1, replica_groups=mesh['req'=8,'tp'=4] {'tp'}, dimensions={1}, use_global_device_ids=true | all-gather | bytes 40960 | tf_op jit(solution)/shard_map/all_gather | solution.py:148
  63.4 39.2 %all-gather.7.cloned.1.call-done = bf16[2048,512]{1,0:T(8,128)(2,1)} async-done(((bf16[256,512]{1,0:T(8,128)(2,1)}), bf16[2048,512]{1,0:T(8,128)(2,1)}) %all-gather.7.cloned.1.call-update) | async-done | bytes 2097168 | tf_op jit(solution)/shard_map/all_gather | solution.py:125
  102.6 3.0 %fusion.68 = f32[512,512]{0,1:T(8,128)S(1)} fusion(bf16[2048,512]{1,0:T(8,128)(2,1)} %all-gather.7.cloned.1.call-done, bf16[512,2048]{1,0:T(8,128)(2,1)S(1)} %copy-done.2, f32[2048]{0:T(1024)S(1)} %convert_element_type.59, f32[512]{0:T(512)S(1)} %add_rsqrt_fusion), kind=kOutput, calls=%fused_computation.120 | convolution fusion | flops 1077936128 | bytes 5253120 | tf_op jit(solution)/shard_map/dot_general | solution.py:123
  105.6 2.3 fusion.12
  107.9 44.7 %all-gather.9.cloned.1.call-done = bf16[2048,512]{1,0:T(8,128)(2,1)} async-done(((bf16[256,512]{1,0:T(8,128)(2,1)}), bf16[2048,512]{1,0:T(8,128)(2,1)}) %all-gather.9.cloned.1.call-update) | async-done | bytes 2097168 | tf_op jit(solution)/shard_map/all_gather | solution.py:115
  152.5 3.9 %fusion.64 = f32[512,512]{0,1:T(8,128)} fusion(bf16[2048,512]{1,0:T(8,128)(2,1)} %all-gather.9.cloned.1.call-done, bf16[512,2048]{1,0:T(8,128)(2,1)S(1)} %copy-done.2, f32[2048]{0:T(1024)S(1)} %convert_element_type.59, f32[512]{0:T(512)S(1)} %add_rsqrt_fusion), kind=kOutput, calls=%fused_computation.119 | convolution fusion | flops 1077936128 | bytes 5253120 | tf_op jit(solution)/shard_map/dot_general | solution.py:113
  156.5 1.9 fusion.9
  158.4 44.0 %all-gather.11.cloned.1.call-done = bf16[2048,512]{1,0:T(8,128)(2,1)} async-done(((bf16[256,512]{1,0:T(8,128)(2,1)}), bf16[2048,512]{1,0:T(8,128)(2,1)}) %all-gather.11.cloned.1.call-update) | async-done | bytes 2097168 | tf_op jit(solution)/shard_map/all_gather | solution.py:120
  202.3 3.0 %fusion.62 = f32[512,512]{0,1:T(8,128)S(1)} fusion(bf16[2048,512]{1,0:T(8,128)(2,1)} %all-gather.11.cloned.1.call-done, bf16[512,2048]{1,0:T(8,128)(2,1)S(1)} %copy-done.2, f32[2048]{0:T(1024)S(1)} %convert_element_type.59, f32[512]{0:T(512)S(1)} %add_rsqrt_fusion), kind=kOutput, calls=%fused_computation.118 | convolution fusion | flops 1077936128 | bytes 5253120 | tf_op jit(solution)/shard_map/dot_general | solution.py:118
  205.4 1.3 subtract_convert_fusion.1
  206.7 8.2 %fusion.72 = (f32[8,512]{1,0:T(8,128)S(1)}, f32[8,512,512]{1,2,0:T(8,128)}) fusion(pred[512,512]{0,1:T(8,128)(4,1)} %fusion.18, bf16[512,8,32]{0,2,1:T(8,128)(2,1)} %get-tuple-element.13, bf16[512,8,32]{0,2,1:T(8,128)(2,1)} %get-tuple-element.14, bf16[512,8,32]{0,2,1:T(8,128)(2,1)} %get-tuple-element.6, bf16[512,8,32]{0,2,1:T(8,128)(2,1)} %get-tuple-element.5), kind=kOutput, calls=%fused_computation.123 | convolution fusion | flops 281018880 | bytes 9715712 | tf_op jit(solution)/shard_map/sub | solution.py:64
  214.9 4.3 %fusion.11 = bf16[8,64,512]{2,1,0:T(8,128)(2,1)S(1)} fusion(bf16[512,8,64]{0,2,1:T(8,128)(2,1)S(1)} %bitcast.46, f32[8,512,512]{1,2,0:T(8,128)} %get-tuple-element.18, f32[8,512]{1,0:T(8,128)S(1)} %get-tuple-element.17), kind=kOutput, calls=%fused_computation.21 | convolution fusion | flops 272891904 | bytes 9453568 | tf_op jit(solution)/shard_map/hqk,khd->qhd/dot_general | solution.py:66
  219.2 34.7 %all-gather.13.cloned.1.call-done = bf16[512,2048]{1,0:T(8,128)(2,1)} async-done(((bf16[512,256]{1,0:T(8,128)(2,1)}), bf16[512,2048]{1,0:T(8,128)(2,1)}) %all-gather.13.cloned.1.call-update) | async-done | bytes 2097168 | tf_op jit(solution)/shard_map/all_gather | solution.py:191
  253.8 4.2 %convolution_convert_fusion = bf16[512,2048]{1,0:T(8,128)(2,1)} fusion(bf16[512,512]{0,1:T(8,128)(2,1)S(1)} %bitcast.51, bf16[512,2048]{1,0:T(8,128)(2,1)} %all-gather.13.cloned.1.call-done), kind=kOutput, calls=%fused_computation.16 | convolution fusion | flops 1074790400 | bytes 4718592 | tf_op jit(solution)/shard_map/dot_general | solution.py:189
  258.1 29.8 %reduce-scatter.2.cloned.1.call-done = bf16[512,512]{1,0:T(8,128)(2,1)} async-done(((bf16[512,2048]{1,0:T(8,128)(2,1)}), bf16[512,512]{1,0:T(8,128)(2,1)}) %reduce-scatter.2.cloned.1.call-update) | async-done | bytes 524304 | tf_op jit(solution)/shard_map/reduce_scatter | solution.py:194
  287.8 2.0 add_convert_fusion
  (57 shorter events, 9.1 us)
Async XLA Ops:
  6.5 1.1 copy-start
  6.5 8.9 %copy-start.6 = (s32[16]{0:T(128)S(1)}, s32[16]{0:T(128)}, u32[]{:S(2)}) copy-start(s32[16]{0:T(128)} %param.15) | copy-start | bytes 196
  6.5 8.2 %copy-start.1 = (s32[16]{0:T(128)S(1)}, s32[16]{0:T(128)}, u32[]{:S(2)}) copy-start(s32[16]{0:T(128)} %param.16) | copy-start | bytes 196
  6.5 8.9 %copy-start.7 = (s32[1,8]{1,0:T(1,128)S(1)}, s32[1,8]{1,0:T(1,128)}, u32[]{:S(2)}) copy-start(s32[1,8]{1,0:T(1,128)} %param.14) | copy-start | bytes 100
  6.5 8.9 %copy-start.5 = (s32[1,512]{1,0:T(1,128)S(1)}, s32[1,512]{1,0:T(1,128)}, u32[]{:S(2)}) copy-start(s32[1,512]{1,0:T(1,128)} %param.13) | copy-start | bytes 6148
  6.5 45.8 %all-gather.15.cloned.1.call-start = ((), (), s32[]{:S(2)}) async-start(), calls=%async_computation.6 | async-start | bytes 1179648 | tf_op jit(solution)/shard_map/all_gather | solution.py:17
  8.5 94.1 %all-gather.7.cloned.1.call-start = ((), (), s32[]{:S(2)}) async-start(), calls=%async_computation.1 | async-start | bytes 2359296 | tf_op jit(solution)/shard_map/all_gather | solution.py:125
  9.3 143.3 %all-gather.9.cloned.1.call-start = ((), (), s32[]{:S(2)}) async-start(), calls=%async_computation.2 | async-start | bytes 2359296 | tf_op jit(solution)/shard_map/all_gather | solution.py:115
  10.0 192.3 %all-gather.11.cloned.1.call-start = ((), (), s32[]{:S(2)}) async-start(), calls=%async_computation.3 | async-start | bytes 2359296 | tf_op jit(solution)/shard_map/all_gather | solution.py:120
  10.6 243.2 %all-gather.13.cloned.1.call-start = ((), (), s32[]{:S(2)}) async-start(), calls=%async_computation.4 | async-start | bytes 2359296 | tf_op jit(solution)/shard_map/all_gather | solution.py:191
  11.2 276.6 %reduce-scatter.2.cloned.1.call-start = ((), (), s32[]{:S(2)}) async-start(), calls=%async_computation.5 | async-start | bytes 2621440 | tf_op jit(solution)/shard_map/reduce_scatter | solution.py:194
  15.4 41.6 %copy-start.2 = (bf16[512,2048]{1,0:T(8,128)(2,1)S(1)}, bf16[512,2048]{1,0:T(8,128)(2,1)}, u32[]{:S(2)}) copy-start(bf16[512,2048]{1,0:T(8,128)(2,1)} %param.12) | copy-start | bytes 6291460
  202.3 3.0 %copy-start.4 = (f32[512,32]{0,1:T(8,128)S(1)}, f32[512,32]{0,1:T(8,128)}, u32[]{:S(2)}) copy-start(f32[512,32]{0,1:T(8,128)} %get-tuple-element.16) | copy-start | bytes 196612
  206.7 8.2 %copy-start.3 = (bf16[512,512]{0,1:T(8,128)(2,1)S(1)}, bf16[512,512]{0,1:T(8,128)(2,1)}, u32[]{:S(2)}) copy-start(bf16[512,512]{0,1:T(8,128)(2,1)} %fusion.12) | copy-start | bytes 1572868
Sparse Core Ops, SparseCore 0:
  9.5 42.8 all-gather.14
  54.5 48.0 all-gather.6
  104.7 47.7 all-gather.8
  154.5 47.7 all-gather.10
  204.2 49.5 all-gather.12
  258.2 29.5 reduce-scatter.1
where the time goes:
time: 297 us
  waiting for transfers between devices  228 us (77%)
  matrix products  31.7 us (11%)
  between operations  13.7 us (5%)
  other arithmetic  10.1 us (3%)
  local copies, waits for them, and re-layouts  7.27 us (2%)
  blocking collectives  5.39 us (2%)
    all_gather x1, waiting for transfers between devices, local(): lax.all_gather(query_weight, 'req', axis=0, tiled=True)  44.7 us
    all_gather x1, waiting for transfers between devices, local(): lax.all_gather(key_weight, 'req', axis=0, tiled=True)  44 us
    all_gather x1, waiting for transfers between devices, local(): lax.all_gather(value_weight, 'req', axis=0, tiled=True)  39.2 us
    all_gather x1, waiting for transfers between devices, local(): lax.all_gather(output_weight, 'req', axis=1, tiled=True)  34.7 us
    all_gather x1, waiting for transfers between devices, fetch_adapters(): fetched = lax.all_gather(stored, 'req', axis=0, tiled=True)  33.5 us
    reduce_scatter x1, waiting for transfers between devices, local(): lax.psum_scatter(partial_out.astype(jnp.bfloat16), 'tp', scatter_dimensio...  29.8 us
    sub x1, matrix products, attend(): scores - row_peak  8.2 us
  transfers between devices with their start and end apart: 6, of which 6 were waited for; matrix products, arithmetic and copies ran while one was open for 14% of the time, Pallas kernels for 0%

commit v1 on v0

--- a/solution.py
+++ b/solution.py
@@ -7,6 +7,22 @@
 norm_eps = 1e-05
 rope_base = 130000.0
 adapter_scale = 2.0
+
+
+def ring_gather(x, axis, dim):
+    ways, here, lap = (lax.axis_size(axis), lax.axis_index(axis), x.shape[dim])
+    shape = [n * ways if d == dim else n for d, n in enumerate(x.shape)]
+    full = lax.dynamic_update_slice_in_dim(jnp.zeros(shape, x.dtype), x, here * lap, axis=dim)
+    going_up = going_down = x
+    for far in range(1, ways // 2 + 1):
+        going_up = lax.ppermute(going_up, axis, [(d, (d + 1) % ways) for d in range(ways)])
+        full = lax.dynamic_update_slice_in_dim(full, going_up, (here - far) % ways * lap, axis=dim)
+        if 2 * far < ways:
+            going_down = lax.ppermute(going_down, axis, [(d, (d - 1) % ways) for d in range(ways)])
+            full = lax.dynamic_update_slice_in_dim(
+                full, going_down, (here + far) % ways * lap, axis=dim
+            )
+    return full
 
 
 def fetch_adapters(down_part, up_part, active_slots, request_adapters, req_total):
@@ -121,9 +137,7 @@
         preferred_element_type=jnp.float32,
     )
     value_plain = jnp.dot(
-        normed,
-        lax.all_gather(value_weight, "req", axis=0, tiled=True),
-        preferred_element_type=jnp.float32,
+        normed, ring_gather(value_weight, "req", 0), preferred_element_type=jnp.float32
     )
     request_total = request_adapters.shape[0]
     member = segment[:, None] == jnp.arange(request_total, dtype=jnp.int32)[None, :]

time: 297 us -> 264 us (0.89)
  waiting for transfers between devices: 228 us -> 170 us
  starting transfers between devices: 0.23 us -> 19.9 us
  local copies, waits for them, and re-layouts: 7.27 us -> 14.2 us
    all_gather x1 -> x0, waiting for transfers between devices: 39.2 us -> none  [local(): lax.all_gather(value_weight, 'req', axis=0, tiled=True)]
    all_gather x1, waiting for transfers between devices: 33.5 us -> 0.01 us  [fetch_adapters(): fetched = lax.all_gather(stored, 'req', axis=0, tiled=True)]
    ppermute x0 -> x7, waiting for transfers between devices: none -> 26.9 us  [the longest x4 24.4 us: ring_gather(): lax.ppermute(going_up, axis, [(d, (d + 1) % ways) for d in range(ways)])]
    ppermute x0 -> x7, starting transfers between devices: none -> 19.7 us  [the longest x4 10.1 us: ring_gather(): lax.ppermute(going_up, axis, [(d, (d + 1) % ways) for d in range(ways)])]
    all_gather x1, waiting for transfers between devices: 44.7 us -> 33.6 us  [local(): lax.all_gather(query_weight, 'req', axis=0, tiled=True)]
    dynamic_update_slice x0 -> x8, local copies, waits for them, and re-layouts: none -> 5.8 us  [the longest x4 2.91 us: ring_gather(): lax.dynamic_update_slice_in_dim(full, going_up, (here - far) % ways * lap...]
  transfers between devices with their start and end apart: 6 -> 12, of which waited for: 6 -> 10; matrix products, arithmetic and copies ran while one was open for 14% -> 17% of each run, Pallas kernels for 0% -> 0%
where the time goes in v1:
time: 264 us; the launch traced here: 263 us
  waiting for transfers between devices  170 us (64%)
  matrix products  31.7 us (12%)
  starting transfers between devices  19.9 us (8%)
  local copies, waits for them, and re-layouts  14.2 us (5%)
  between operations  13.5 us (5%)
  other arithmetic  7.84 us (3%)
  blocking collectives  5.38 us (2%)
    all_gather x1, waiting for transfers between devices, local(): lax.all_gather(key_weight, 'req', axis=0, tiled=True)  44.1 us
    all_gather x1, waiting for transfers between devices, local(): lax.all_gather(output_weight, 'req', axis=1, tiled=True)  34.7 us
    all_gather x1, waiting for transfers between devices, local(): lax.all_gather(query_weight, 'req', axis=0, tiled=True)  33.6 us
    reduce_scatter x1, waiting for transfers between devices, local(): lax.psum_scatter(partial_out.astype(jnp.bfloat16), 'tp', scatter_dimensio...  29.8 us
    ppermute x4, waiting for transfers between devices, ring_gather(): lax.ppermute(going_up, axis, [(d, (d + 1) % ways) for d in range(ways)])  24.4 us
    ppermute x4, starting transfers between devices, ring_gather(): lax.ppermute(going_up, axis, [(d, (d + 1) % ways) for d in range(ways)])  10.1 us
    ppermute x3, starting transfers between devices, ring_gather(): lax.ppermute(going_down, axis, [(d, (d - 1) % ways) for d in range(ways)])  9.61 us
    sub x1, matrix products, attend(): scores - row_peak  8.19 us
  transfers between devices with their start and end apart: 12, of which 10 were waited for; matrix products, arithmetic and copies ran while one was open for 17% of the time, Pallas kernels for 0%

profile of v1, /device:TPU:0, one launch (start us, length us, event | category | flops | bytes accessed | tf_op | source)
XLA Modules:
  0.0 263.0 jit_solution(12286068557097191979)
XLA Ops:
  10.1 3.0 %collective-permute-start = (bf16[256,512]{1,0:T(8,128)(2,1)}, bf16[256,512]{1,0:T(8,128)(2,1)S(1)}, u32[]{:S(2)}, u32[]{:S(2)}) collective-permute-start(bf16[256,512]{1,0:T(8,128)(2,1)} %param.20), channel_id=1, source_target_pairs={{0,4},{4,8},{8,12},{12,16},{16,20},{20,24},{24,28},{28,0},{1,5},{5... | collective-permute-start | bytes 786440 | tf_op jit(solution)/shard_map/ppermute | solution.py:18
  13.2 3.1 %collective-permute-start.1 = (bf16[256,512]{1,0:T(8,128)(2,1)}, bf16[256,512]{1,0:T(8,128)(2,1)S(1)}, u32[]{:S(2)}, u32[]{:S(2)}) collective-permute-start(bf16[256,512]{1,0:T(8,128)(2,1)} %param.20), channel_id=1, source_target_pairs={{0,28},{4,0},{8,4},{12,8},{16,12},{20,16},{24,20},{28,24},{1,29},{... | collective-permute-start | bytes 786440 | tf_op jit(solution)/shard_map/ppermute | solution.py:21
  22.3 3.7 %collective-permute-done = bf16[256,512]{1,0:T(8,128)(2,1)S(1)} collective-permute-done((bf16[256,512]{1,0:T(8,128)(2,1)}, bf16[256,512]{1,0:T(8,128)(2,1)S(1)}, u32[]{:S(2)}, u32[]{:S(2)}) %collective-permute-start) | collective-permute-done | bytes 262176 | tf_op jit(solution)/shard_map/ppermute | solution.py:18
  26.1 2.4 collective-permute-start.2
  30.6 3.0 %collective-permute-start.3 = (bf16[256,512]{1,0:T(8,128)(2,1)S(1)}, bf16[256,512]{1,0:T(8,128)(2,1)S(1)}, u32[]{:S(2)}, u32[]{:S(2)}) collective-permute-start(bf16[256,512]{1,0:T(8,128)(2,1)S(1)} %collective-permute-done.1), channel_id=1, source_target_pairs={{0,28},{4,0},{8,4},{12,8},{16,12},{20,16},{24,20},{28,24},{1,29},{... | collective-permute-start | bytes 786440 | tf_op jit(solution)/shard_map/ppermute | solution.py:21
  33.9 5.2 %collective-permute-done.2 = bf16[256,512]{1,0:T(8,128)(2,1)S(1)} collective-permute-done((bf16[256,512]{1,0:T(8,128)(2,1)S(1)}, bf16[256,512]{1,0:T(8,128)(2,1)S(1)}, u32[]{:S(2)}, u32[]{:S(2)}) %collective-permute-start.2) | collective-permute-done | bytes 262176 | tf_op jit(solution)/shard_map/ppermute | solution.py:18
  39.0 2.2 collective-permute-start.4
  43.0 3.5 %collective-permute-start.5 = (bf16[256,512]{1,0:T(8,128)(2,1)S(1)}, bf16[256,512]{1,0:T(8,128)(2,1)S(1)}, u32[]{:S(2)}, u32[]{:S(2)}) collective-permute-start(bf16[256,512]{1,0:T(8,128)(2,1)S(1)} %collective-permute-done.3), channel_id=1, source_target_pairs={{0,28},{4,0},{8,4},{12,8},{16,12},{20,16},{24,20},{28,24},{1,29},{... | collective-permute-start | bytes 786440 | tf_op jit(solution)/shard_map/ppermute | solution.py:21
  47.2 10.2 %collective-permute-done.4 = bf16[256,512]{1,0:T(8,128)(2,1)S(1)} collective-permute-done((bf16[256,512]{1,0:T(8,128)(2,1)S(1)}, bf16[256,512]{1,0:T(8,128)(2,1)S(1)}, u32[]{:S(2)}, u32[]{:S(2)}) %collective-permute-start.4) | collective-permute-done | bytes 262176 | tf_op jit(solution)/shard_map/ppermute | solution.py:18
  57.4 2.5 collective-permute-start.6
  61.4 2.2 collective-permute-done.5
  64.3 5.2 %collective-permute-done.6 = bf16[256,512]{1,0:T(8,128)(2,1)S(1)} collective-permute-done((bf16[256,512]{1,0:T(8,128)(2,1)S(1)}, bf16[256,512]{1,0:T(8,128)(2,1)S(1)}, u32[]{:S(2)}, u32[]{:S(2)}) %collective-permute-start.6) | collective-permute-done | bytes 262176 | tf_op jit(solution)/shard_map/ppermute | solution.py:18
  74.8 5.4 %all_gather.16 = bf16[512,32]{0,1:T(8,128)(2,1)S(1)} all-gather(bf16[512,8]{0,1:T(8,128)(2,1)S(1)} %fusion.16), channel_id=1, replica_groups=mesh['req'=8,'tp'=4] {'tp'}, dimensions={1}, use_global_device_ids=true | all-gather | bytes 40960 | tf_op jit(solution)/shard_map/all_gather | solution.py:162
  81.7 3.8 %fusion.11 = bf16[512,512]{0,1:T(8,128)(2,1)} fusion(f32[512,512]{0,1:T(8,128)S(1)} %convolution_multiply_fusion.1, bf16[2048,512]{1,0:T(8,128)(2,1)} %constant_dynamic-update-slice_fusion, bf16[512,2048]{1,0:T(8,128)(2,1)S(1)} %copy-done.1, f32[2048]{0:T(1024)S(1)} %convert_element_type.59, f32[512]{0:T(512)S(1)} %add_rsqrt_fusion), kind=kOutput, calls=%fused_computation.22 | convolution fusion | flops 1078460416 | bytes 5777408 | tf_op jit(solution)/shard_map/dot_general | solution.py:139
  85.5 33.6 %all-gather.6.cloned.1.call-done = bf16[2048,512]{1,0:T(8,128)(2,1)} async-done(((bf16[256,512]{1,0:T(8,128)(2,1)}), bf16[2048,512]{1,0:T(8,128)(2,1)}) %all-gather.6.cloned.1.call-update) | async-done | bytes 2097168 | tf_op jit(solution)/shard_map/all_gather | solution.py:131
  119.1 3.9 %fusion.63 = f32[512,512]{0,1:T(8,128)} fusion(bf16[2048,512]{1,0:T(8,128)(2,1)} %all-gather.6.cloned.1.call-done, bf16[512,2048]{1,0:T(8,128)(2,1)S(1)} %copy-done.1, f32[2048]{0:T(1024)S(1)} %convert_element_type.59, f32[512]{0:T(512)S(1)} %add_rsqrt_fusion), kind=kOutput, calls=%fused_computation.127 | convolution fusion | flops 1077936128 | bytes 5253120 | tf_op jit(solution)/shard_map/dot_general | solution.py:129
  124.9 44.1 %all-gather.8.cloned.1.call-done = bf16[2048,512]{1,0:T(8,128)(2,1)} async-done(((bf16[256,512]{1,0:T(8,128)(2,1)}), bf16[2048,512]{1,0:T(8,128)(2,1)}) %all-gather.8.cloned.1.call-update) | async-done | bytes 2097168 | tf_op jit(solution)/shard_map/all_gather | solution.py:136
  169.0 3.0 %fusion.61 = f32[512,512]{0,1:T(8,128)S(1)} fusion(bf16[2048,512]{1,0:T(8,128)(2,1)} %all-gather.8.cloned.1.call-done, bf16[512,2048]{1,0:T(8,128)(2,1)S(1)} %copy-done.1, f32[2048]{0:T(1024)S(1)} %convert_element_type.59, f32[512]{0:T(512)S(1)} %add_rsqrt_fusion), kind=kOutput, calls=%fused_computation.126 | convolution fusion | flops 1077936128 | bytes 5253120 | tf_op jit(solution)/shard_map/dot_general | solution.py:134
  173.3 8.2 %fusion.70 = (f32[8,512]{1,0:T(8,128)S(1)}, f32[8,512,512]{1,2,0:T(8,128)}) fusion(pred[512,512]{0,1:T(8,128)(4,1)} %fusion.17, bf16[512,8,32]{0,2,1:T(8,128)(2,1)} %get-tuple-element.13, bf16[512,8,32]{0,2,1:T(8,128)(2,1)} %get-tuple-element.14, bf16[512,8,32]{0,2,1:T(8,128)(2,1)} %get-tuple-element.6, bf16[512,8,32]{0,2,1:T(8,128)(2,1)} %get-tuple-element.5), kind=kOutput, calls=%fused_computation.130 | convolution fusion | flops 281018880 | bytes 9715712 | tf_op jit(solution)/shard_map/sub | solution.py:80
  181.5 4.2 %fusion.10 = bf16[8,64,512]{2,1,0:T(8,128)(2,1)S(1)} fusion(bf16[512,8,64]{0,2,1:T(8,128)(2,1)S(1)} %bitcast.50, f32[8,512,512]{1,2,0:T(8,128)} %get-tuple-element.18, f32[8,512]{1,0:T(8,128)S(1)} %get-tuple-element.17), kind=kOutput, calls=%fused_computation.21 | convolution fusion | flops 272891904 | bytes 9453568 | tf_op jit(solution)/shard_map/hqk,khd->qhd/dot_general | solution.py:82
  185.8 34.7 %all-gather.10.cloned.1.call-done = bf16[512,2048]{1,0:T(8,128)(2,1)} async-done(((bf16[512,256]{1,0:T(8,128)(2,1)}), bf16[512,2048]{1,0:T(8,128)(2,1)}) %all-gather.10.cloned.1.call-update) | async-done | bytes 2097168 | tf_op jit(solution)/shard_map/all_gather | solution.py:205
  220.5 4.2 %convolution_convert_fusion = bf16[512,2048]{1,0:T(8,128)(2,1)} fusion(bf16[512,512]{0,1:T(8,128)(2,1)S(1)} %bitcast.51, bf16[512,2048]{1,0:T(8,128)(2,1)} %all-gather.10.cloned.1.call-done), kind=kOutput, calls=%fused_computation.16 | convolution fusion | flops 1074790400 | bytes 4718592 | tf_op jit(solution)/shard_map/dot_general | solution.py:203
  224.7 29.8 %reduce-scatter.2.cloned.1.call-done = bf16[512,512]{1,0:T(8,128)(2,1)} async-done(((bf16[512,2048]{1,0:T(8,128)(2,1)}), bf16[512,512]{1,0:T(8,128)(2,1)}) %reduce-scatter.2.cloned.1.call-update) | async-done | bytes 524304 | tf_op jit(solution)/shard_map/reduce_scatter | solution.py:208
  254.5 2.0 add_convert_fusion
  (81 shorter events, 26.4 us)
Async XLA Ops:
  6.5 1.1 copy-start
  6.5 11.8 %copy-start.7 = (s32[16]{0:T(128)S(1)}, s32[16]{0:T(128)}, u32[]{:S(2)}) copy-start(s32[16]{0:T(128)} %param.15) | copy-start | bytes 196
  6.5 11.8 %copy-start.8 = (s32[1,8]{1,0:T(1,128)S(1)}, s32[1,8]{1,0:T(1,128)}, u32[]{:S(2)}) copy-start(s32[1,8]{1,0:T(1,128)} %param.14) | copy-start | bytes 100
  6.5 11.9 %copy-start.1 = (bf16[512,2048]{1,0:T(8,128)(2,1)S(1)}, bf16[512,2048]{1,0:T(8,128)(2,1)}, u32[]{:S(2)}) copy-start(bf16[512,2048]{1,0:T(8,128)(2,1)} %param.12) | copy-start | bytes 6291460
  6.5 63.7 %all-gather.12.cloned.1.call-start = ((), (), s32[]{:S(2)}) async-start(), calls=%async_computation.5 | async-start | bytes 1179648 | tf_op jit(solution)/shard_map/all_gather | solution.py:33
  6.6 12.3 %copy-start.5 = (s32[1,512]{1,0:T(1,128)S(1)}, s32[1,512]{1,0:T(1,128)}, u32[]{:S(2)}) copy-start(s32[1,512]{1,0:T(1,128)} %param.13) | copy-start | bytes 6148
  8.6 110.5 %all-gather.6.cloned.1.call-start = ((), (), s32[]{:S(2)}) async-start(), calls=%async_computation.1 | async-start | bytes 2359296 | tf_op jit(solution)/shard_map/all_gather | solution.py:131
  9.4 159.6 %all-gather.8.cloned.1.call-start = ((), (), s32[]{:S(2)}) async-start(), calls=%async_computation.2 | async-start | bytes 2359296 | tf_op jit(solution)/shard_map/all_gather | solution.py:136
  10.1 210.4 %all-gather.10.cloned.1.call-start = ((), (), s32[]{:S(2)}) async-start(), calls=%async_computation.3 | async-start | bytes 2359296 | tf_op jit(solution)/shard_map/all_gather | solution.py:205
  10.1 15.9 %collective-permute-start = (bf16[256,512]{1,0:T(8,128)(2,1)}, bf16[256,512]{1,0:T(8,128)(2,1)S(1)}, u32[]{:S(2)}, u32[]{:S(2)}) collective-permute-start(bf16[256,512]{1,0:T(8,128)(2,1)} %param.20), channel_id=1, source_target_pairs={{0,4},{4,8},{8,12},{12,16},{16,20},{20,24},{24,28},{28,0},{1,5},{5... | collective-permute-start | bytes 786440 | tf_op jit(solution)/shard_map/ppermute | solution.py:18
  13.2 17.5 %collective-permute-start.1 = (bf16[256,512]{1,0:T(8,128)(2,1)}, bf16[256,512]{1,0:T(8,128)(2,1)S(1)}, u32[]{:S(2)}, u32[]{:S(2)}) collective-permute-start(bf16[256,512]{1,0:T(8,128)(2,1)} %param.20), channel_id=1, source_target_pairs={{0,28},{4,0},{8,4},{12,8},{16,12},{20,16},{24,20},{28,24},{1,29},{... | collective-permute-start | bytes 786440 | tf_op jit(solution)/shard_map/ppermute | solution.py:21
  16.3 238.2 %reduce-scatter.2.cloned.1.call-start = ((), (), s32[]{:S(2)}) async-start(), calls=%async_computation.4 | async-start | bytes 2621440 | tf_op jit(solution)/shard_map/reduce_scatter | solution.py:208
  18.4 11.5 %copy-start.3 = (bf16[256,512]{1,0:T(8,128)(2,1)S(1)}, bf16[256,512]{1,0:T(8,128)(2,1)}, u32[]{:S(2)}) copy-start(bf16[256,512]{1,0:T(8,128)(2,1)} %param.20) | copy-start | bytes 786436
  18.9 14.9 %copy-start.6 = (bf16[2048]{0:T(1024)(128)(2,1)S(1)}, bf16[2048]{0:T(1024)(128)(2,1)}, u32[]{:S(2)}) copy-start(bf16[2048]{0:T(1024)(128)(2,1)} %param.17) | copy-start | bytes 12292
  26.1 13.0 %collective-permute-start.2 = (bf16[256,512]{1,0:T(8,128)(2,1)S(1)}, bf16[256,512]{1,0:T(8,128)(2,1)S(1)}, u32[]{:S(2)}, u32[]{:S(2)}) collective-permute-start(bf16[256,512]{1,0:T(8,128)(2,1)S(1)} %collective-permute-done), channel_id=1, source_target_pairs={{0,4},{4,8},{8,12},{12,16},{16,20},{20,24},{24,28},{28,0},{1,5},{5... | collective-permute-start | bytes 786440 | tf_op jit(solution)/shard_map/ppermute | solution.py:18
  30.6 12.3 %collective-permute-start.3 = (bf16[256,512]{1,0:T(8,128)(2,1)S(1)}, bf16[256,512]{1,0:T(8,128)(2,1)S(1)}, u32[]{:S(2)}, u32[]{:S(2)}) collective-permute-start(bf16[256,512]{1,0:T(8,128)(2,1)S(1)} %collective-permute-done.1), channel_id=1, source_target_pairs={{0,28},{4,0},{8,4},{12,8},{16,12},{20,16},{24,20},{28,24},{1,29},{... | collective-permute-start | bytes 786440 | tf_op jit(solution)/shard_map/ppermute | solution.py:21
  39.0 18.4 %collective-permute-start.4 = (bf16[256,512]{1,0:T(8,128)(2,1)S(1)}, bf16[256,512]{1,0:T(8,128)(2,1)S(1)}, u32[]{:S(2)}, u32[]{:S(2)}) collective-permute-start(bf16[256,512]{1,0:T(8,128)(2,1)S(1)} %collective-permute-done.2), channel_id=1, source_target_pairs={{0,4},{4,8},{8,12},{12,16},{16,20},{20,24},{24,28},{28,0},{1,5},{5... | collective-permute-start | bytes 786440 | tf_op jit(solution)/shard_map/ppermute | solution.py:18
  43.0 20.6 %collective-permute-start.5 = (bf16[256,512]{1,0:T(8,128)(2,1)S(1)}, bf16[256,512]{1,0:T(8,128)(2,1)S(1)}, u32[]{:S(2)}, u32[]{:S(2)}) collective-permute-start(bf16[256,512]{1,0:T(8,128)(2,1)S(1)} %collective-permute-done.3), channel_id=1, source_target_pairs={{0,28},{4,0},{8,4},{12,8},{16,12},{20,16},{24,20},{28,24},{1,29},{... | collective-permute-start | bytes 786440 | tf_op jit(solution)/shard_map/ppermute | solution.py:21
  57.4 12.1 %collective-permute-start.6 = (bf16[256,512]{1,0:T(8,128)(2,1)S(1)}, bf16[256,512]{1,0:T(8,128)(2,1)S(1)}, u32[]{:S(2)}, u32[]{:S(2)}) collective-permute-start(bf16[256,512]{1,0:T(8,128)(2,1)S(1)} %collective-permute-done.4), channel_id=1, source_target_pairs={{0,4},{4,8},{8,12},{12,16},{16,20},{20,24},{24,28},{28,0},{1,5},{5... | collective-permute-start | bytes 786440 | tf_op jit(solution)/shard_map/ppermute | solution.py:18
  72.6 1.0 copy-start.2
  169.0 3.0 %copy-start.4 = (f32[512,32]{0,1:T(8,128)S(1)}, f32[512,32]{0,1:T(8,128)}, u32[]{:S(2)}) copy-start(f32[512,32]{0,1:T(8,128)} %get-tuple-element.16) | copy-start | bytes 196612
  173.3 8.2 %copy-start.9 = (bf16[512,512]{0,1:T(8,128)(2,1)S(1)}, bf16[512,512]{0,1:T(8,128)(2,1)}, u32[]{:S(2)}) copy-start(bf16[512,512]{0,1:T(8,128)(2,1)} %fusion.11) | copy-start | bytes 1572868
Sparse Core Ops, SparseCore 0:
  9.5 58.7 all-gather.11
  70.4 48.5 all-gather.5
  121.2 47.7 all-gather.7
  170.9 49.5 all-gather.9
  224.8 29.5 reduce-scatter.1
